TPU v7x, 32 devices: a whole 2x2x4 slice. The times are simulated.
32 devices in a mesh: seq: 8 (over z, y), tensor: 4 (over x, core).
Axes of the slice: x: 2, y: 2, z: 4, core: 2. Of those that a mesh axis runs over, the one named last changes fastest.
Arguments:
- residual: bfloat16 [4608, 6144], P('seq', 'tensor'), may hold values from -4 to 4
- queries: bfloat16 [4608, 4096], P(('seq', 'tensor')), may hold values from -6 to 6
- key_rows: bfloat16 [4608, 4096], P(('seq', 'tensor')), may hold values from -6 to 6
- value_rows: bfloat16 [4608, 4096], P(('seq', 'tensor')), may hold values from -6 to 6
- w_out: bfloat16 [4096, 6144], P(None, 'tensor'), may hold values from -0.09375 to 0.09375
- out_gate: float32 [6144], P('tensor'), may hold values from 0.5 to 1.5
- extents: int32 [32, 3], replicated, may hold values from 0 to 1, as said below
Outputs:
- updated: bfloat16 [4608, 6144], P('seq', 'tensor')
Inputs may be any that keep to these rules, and one draw needn't show every extreme that they name: `extents`: reaches in tile-frames are at most 1, in tile-rows at most 1, in tile-columns at most 1; each of these bounds is taken by some head, and some head has reach 0 in tile-rows.
All inputs are finite; a program needn't handle non-finite values.
Results may differ from a plain program's by a relative error of at most 0.0048.
Values may be sent and summed in bfloat16 or wider, within the bound.
A program may use at most 192 MiB of HBM per device.

v0:
```python
import math
import jax
import jax.numpy as jnp
from jax import lax
from jax.sharding import PartitionSpec as P

HEAD_DIM = 128
TILE = 32
HT_DEV = 2
WT = 3


def passed_along(value, axis, by):
    length = lax.axis_size(axis)
    pairs = [(i, i + by) for i in range(length) if 0 <= i + by < length]
    return lax.ppermute(value, axis, pairs)


def tile_coords(row_count, tile_rows, first_row):
    position = jnp.arange(row_count, dtype=jnp.int32)
    frame_id = position // (tile_rows * WT * TILE)
    row_id = first_row + position // (WT * TILE) % tile_rows
    col_id = position // TILE % WT
    return (frame_id, row_id, col_id)


def allowed_keys(query_place, key_place, head_reach, seq_block, seq_count):
    frame_gap = jnp.abs(query_place[0][:, None] - key_place[0][None, :])
    row_gap = jnp.abs(query_place[1][:, None] - key_place[1][None, :])
    col_gap = jnp.abs(query_place[2][:, None] - key_place[2][None, :])
    global_row = key_place[1] + seq_block * HT_DEV
    inside = (global_row >= 0) & (global_row < seq_count * HT_DEV)
    return (
        (frame_gap[None] <= head_reach[:, 0, None, None])
        & (row_gap[None] <= head_reach[:, 1, None, None])
        & (col_gap[None] <= head_reach[:, 2, None, None])
        & inside[None, None, :]
    )


def shards(residual, queries, key_rows, value_rows, w_out, out_gate, extents):
    head_q, head_k, head_v = (
        lax.all_to_all(queries, "tensor", split_axis=1, concat_axis=0, tiled=True),
        lax.all_to_all(key_rows, "tensor", split_axis=1, concat_axis=0, tiled=True),
        lax.all_to_all(value_rows, "tensor", split_axis=1, concat_axis=0, tiled=True),
    )
    tokens = head_q.shape[0]
    inner_dev = head_q.shape[1]
    head_dim = HEAD_DIM
    heads_here = inner_dev // head_dim
    seq_block = lax.axis_index("seq")
    seq_count = lax.axis_size("seq")
    head_reach = lax.dynamic_slice_in_dim(
        extents, lax.axis_index("tensor") * heads_here, heads_here, 0
    )
    query_tiles = head_q.reshape(tokens, heads_here, head_dim)
    query_place = tile_coords(tokens, HT_DEV, 0)
    stacked = jnp.stack([head_k, head_v])

    def part_scores(pair_rows, key_place):
        key_tiles = pair_rows[0].reshape(-1, heads_here, head_dim)
        scores = jnp.einsum(
            "qhd,khd->hqk", query_tiles, key_tiles, preferred_element_type=jnp.float32
        ) / math.sqrt(head_dim)
        allowed = allowed_keys(query_place, key_place, head_reach, seq_block, seq_count)
        return jnp.where(allowed, scores, -1e30)

    lower_part = passed_along(stacked, "seq", 1)
    upper_part = passed_along(stacked, "seq", -1)
    remote = [
        (lower_part, tile_coords(tokens, HT_DEV, -HT_DEV)),
        (upper_part, tile_coords(tokens, HT_DEV, HT_DEV)),
    ]
    own_scores = part_scores(stacked, query_place)
    scores = jnp.concatenate(
        [own_scores] + [part_scores(pair_rows, key_place) for pair_rows, key_place in remote],
        axis=-1,
    )
    value_all = jnp.concatenate(
        [stacked[1]] + [pair_rows[1] for pair_rows, key_place in remote], axis=0
    )
    row_max = jnp.max(scores, axis=-1, keepdims=True)
    exp_scores = jnp.exp(scores - row_max)
    row_sum = jnp.sum(exp_scores, axis=-1, keepdims=True)
    weights = (exp_scores / row_sum).astype(jnp.bfloat16)
    attended = jnp.einsum(
        "hqk,khd->qhd",
        weights,
        value_all.reshape(-1, heads_here, head_dim),
        preferred_element_type=jnp.float32,
    )
    head_out = attended.reshape(tokens, inner_dev).astype(jnp.bfloat16)
    projected = jnp.dot(
        lax.all_gather(head_out, "tensor", axis=1, tiled=True),
        w_out,
        preferred_element_type=jnp.float32,
    )
    return (residual.astype(jnp.float32) + out_gate * projected).astype(jnp.bfloat16)


def solution(mesh):
    placed = (
        P("seq", "tensor"),
        P(("seq", "tensor"), None),
        P(("seq", "tensor"), None),
        P(("seq", "tensor"), None),
        P(None, "tensor"),
        P("tensor"),
        P(),
    )
    return jax.shard_map(
        shards, mesh=mesh, in_specs=placed, out_specs=P("seq", "tensor"), check_vma=False
    )
```

profile of v0, /device:TPU:0, one launch (start us, length us, event | category | flops | bytes accessed | tf_op | source)
XLA Modules:
  0.0 309.6 jit_solution(9259472700142970301)
XLA Ops:
  6.5 2.5 copy.92
  9.1 4.2 %all-to-all-start.1 = ((bf16[144,4,1024]{2,0,1:T(8,128)(2,1)}), bf16[144,4,1024]{2,0,1:T(8,128)(2,1)S(1)}, u32[]{:S(2)}, u32[]{:S(2)}) async-start(bf16[144,4,1024]{2,0,1:T(8,128)(2,1)} %bitcast.60), calls=%async_computation.1 | async-start | bytes 2359296 | tf_op jit(solution)/shard_map/all_to_all | solution.py:44
  13.3 1.1 copy.91
  14.4 14.7 %all-to-all-done.1 = bf16[144,4,1024]{2,0,1:T(8,128)(2,1)S(1)} async-done(((bf16[144,4,1024]{2,0,1:T(8,128)(2,1)}), bf16[144,4,1024]{2,0,1:T(8,128)(2,1)S(1)}, u32[]{:S(2)}, u32[]{:S(2)}) %all-to-all-start.1) | async-done | bytes 1179680 | tf_op jit(solution)/shard_map/all_to_all | solution.py:44
  29.1 3.5 %all-to-all-start = ((bf16[144,4,1024]{2,0,1:T(8,128)(2,1)}), bf16[144,4,1024]{2,0,1:T(8,128)(2,1)S(1)}, u32[]{:S(2)}, u32[]{:S(2)}) async-start(bf16[144,4,1024]{2,0,1:T(8,128)(2,1)} %bitcast.59), calls=%async_computation | async-start | bytes 2359296 | tf_op jit(solution)/shard_map/all_to_all | solution.py:45
  32.7 1.1 copy.93
  33.9 14.7 %all-to-all-done = bf16[144,4,1024]{2,0,1:T(8,128)(2,1)S(1)} async-done(((bf16[144,4,1024]{2,0,1:T(8,128)(2,1)}), bf16[144,4,1024]{2,0,1:T(8,128)(2,1)S(1)}, u32[]{:S(2)}, u32[]{:S(2)}) %all-to-all-start) | async-done | bytes 1179680 | tf_op jit(solution)/shard_map/all_to_all | solution.py:45
  48.5 3.5 %all-to-all-start.2 = ((bf16[144,4,1024]{2,0,1:T(8,128)(2,1)}), bf16[144,4,1024]{2,0,1:T(8,128)(2,1)S(1)}, u32[]{:S(2)}, u32[]{:S(2)}) async-start(bf16[144,4,1024]{2,0,1:T(8,128)(2,1)} %bitcast.61), calls=%async_computation.2 | async-start | bytes 2359296 | tf_op jit(solution)/shard_map/all_to_all | solution.py:43
  52.0 0.0 all-gather.2.cloned.1.call-start
  52.1 1.6 pad_maximum_fusion
  53.7 1.3 collective-permute-start.1
  55.0 0.6 compare_and_fusion.6
  55.7 6.2 %collective-permute-start = (bf16[2,576,1024]{2,1,0:T(8,128)(2,1)}, bf16[2,576,1024]{2,1,0:T(8,128)(2,1)}, u32[]{:S(2)}, u32[]{:S(2)}) collective-permute-start(bf16[2,576,1024]{2,1,0:T(8,128)(2,1)} %pad_maximum_fusion), channel_id=1, source_target_pairs={{0,4},{4,8},{8,12},{12,16},{16,20},{20,24},{24,28},{1,5},{5,9},{9,... | collective-permute-start | bytes 7077896 | tf_op jit(solution)/shard_map/ppermute | solution.py:16
  61.9 0.1 constant_dynamic-slice_fusion
  62.0 0.5 compare_and_fusion.8
  62.5 0.6 slice_bitcast_fusion.5
  63.1 2.0 subtract_abs_fusion.2
  65.2 2.7 subtract_abs_fusion
  67.9 0.3 copy.55
  68.2 0.3 copy.56
  68.5 0.0 copy-start.2
  68.6 0.3 copy.59
  68.9 0.2 copy.39
  69.1 0.8 copy-done.2
  69.9 0.4 copy-done.3
  70.4 0.4 copy-done.6
  70.8 8.3 %fusion.36 = (f32[8,576]{1,0:T(8,128)S(1)}, f32[8,576,576]{2,1,0:T(8,128)}) fusion(bf16[576,8,128]{2,1,0:T(8,128)(2,1)S(1)} %bitcast.79, bf16[576,8,128]{2,1,0:T(8,128)(2,1)S(1)} %bitcast.74, pred[576]{0:T(1024)(128)(4,1)S(1)} %copy-done.17, s32[8]{0:T(128)S(1)} %copy-done.13, s32[576,576]{1,0:T(8,128)S(1)} %copy-done.2, s32[8]{0:T(128)S(1)} %get-tuple-element.12, ...), kind=kOutput, calls=%fused_computation.83 | convolution fusion | flops 703360512 | bytes 16976544 | tf_op jit(solution)/shard_map/qhd,khd->hqk/dot_general | solution.py:62
  79.1 30.9 %collective-permute-done.1 = bf16[2,576,1024]{2,1,0:T(8,128)(2,1)} collective-permute-done((bf16[2,576,1024]{2,1,0:T(8,128)(2,1)}, bf16[2,576,1024]{2,1,0:T(8,128)(2,1)}, u32[]{:S(2)}, u32[]{:S(2)}) %collective-permute-start.1) | collective-permute-done | bytes 2359328 | tf_op jit(solution)/shard_map/ppermute | solution.py:16
  110.0 2.1 slice_bitcast_fusion.2
  112.1 0.3 copy.58
  112.5 0.3 copy.61
  112.8 0.2 copy.41
  113.0 47.8 %collective-permute-done = bf16[2,576,1024]{2,1,0:T(8,128)(2,1)} collective-permute-done((bf16[2,576,1024]{2,1,0:T(8,128)(2,1)}, bf16[2,576,1024]{2,1,0:T(8,128)(2,1)}, u32[]{:S(2)}, u32[]{:S(2)}) %collective-permute-start) | collective-permute-done | bytes 2359328 | tf_op jit(solution)/shard_map/ppermute | solution.py:16
  160.8 2.1 slice_bitcast_fusion.3
  162.9 0.3 copy.57
  163.2 0.3 copy.60
  163.5 0.2 copy.40
  163.7 0.9 copy-done.5
  164.6 8.1 %fusion.35 = (f32[8,576]{1,0:T(8,128)S(1)}, f32[8,576,576]{2,1,0:T(8,128)}) fusion(bf16[576,8,128]{2,1,0:T(8,128)(2,1)S(1)} %bitcast.75, bf16[576,8,128]{2,1,0:T(8,128)(2,1)S(1)} %bitcast.77, pred[576]{0:T(1024)(128)(4,1)S(1)} %copy-done.10, s32[8]{0:T(128)S(1)} %copy-done.13, s32[576,576]{1,0:T(8,128)S(1)} %copy-done.2, s32[8]{0:T(128)S(1)} %copy-done.12, ...), kind=kOutput, calls=%fused_computation.82 | convolution fusion | flops 703360512 | bytes 16976544 | tf_op jit(solution)/shard_map/qhd,khd->hqk/dot_general | solution.py:62
  172.7 8.1 %fusion.37 = (f32[8,576]{1,0:T(8,128)S(1)}, f32[8,576,576]{2,1,0:T(8,128)}) fusion(bf16[576,8,128]{2,1,0:T(8,128)(2,1)S(1)} %bitcast.76, bf16[576,8,128]{2,1,0:T(8,128)(2,1)S(1)} %bitcast.78, pred[576]{0:T(1024)(128)(4,1)S(1)} %copy-done.9, s32[8]{0:T(128)S(1)} %copy-done.13, s32[576,576]{1,0:T(8,128)S(1)} %copy-done.2, s32[8]{0:T(128)S(1)} %copy-done.12, ...), kind=kOutput, calls=%fused_computation.84 | convolution fusion | flops 703360512 | bytes 16976544 | tf_op jit(solution)/shard_map/qhd,khd->hqk/dot_general | solution.py:62
  180.8 0.6 maximum_maximum_fusion
  181.4 36.3 %concatenate.17 = f32[8,576,1728]{2,1,0:T(8,128)} concatenate(f32[8,576,576]{2,1,0:T(8,128)} %get-tuple-element.18, f32[8,576,576]{2,1,0:T(8,128)} %get-tuple-element.20, f32[8,576,576]{2,1,0:T(8,128)} %get-tuple-element.16), dimensions={2} | concatenate | bytes 63700992 | tf_op jit(solution)/shard_map/concatenate | solution.py:75
  217.7 14.1 %fusion = f32[8,576]{1,0:T(8,128)} fusion(f32[8,576,1728]{2,1,0:T(8,128)} %concatenate.17, f32[8,576]{1,0:T(8,128)} %maximum_maximum_fusion), kind=kLoop, calls=%fused_computation.2 | loop fusion | flops 15920640 | bytes 31887360 | tf_op jit(solution)/shard_map/reduce_sum | solution.py:84
  231.8 14.3 %fusion.13 = bf16[8,72,8,128]{3,2,1,0:T(8,128)(2,1)} fusion(bf16[576,8,128]{2,0,1:T(8,128)(2,1)S(1)} %copy.41, bf16[576,8,128]{2,0,1:T(8,128)(2,1)S(1)} %copy.40, bf16[576,8,128]{2,0,1:T(8,128)(2,1)S(1)} %copy.39, f32[8,576,1728]{2,1,0:T(8,128)} %concatenate.17, f32[8,576]{1,0:T(8,128)} %fusion, f32[8,576]{1,0:T(8,128)} %maximum_maximum_fusion), kind=kOutput, calls=%fused_computation.30 | convolution fusion | flops 2073526272 | bytes 36605952 | tf_op jit(solution)/shard_map/hqk,khd->qhd/dot_general | solution.py:86
  246.1 2.8 copy.90
  248.9 0.0 all-gather.2.cloned.1.call-update
  248.9 41.1 %all-gather.2.cloned.1.call-done = bf16[576,4096]{1,0:T(8,128)(2,1)} async-done(((bf16[576,1024]{1,0:T(8,128)(2,1)}), bf16[576,4096]{1,0:T(8,128)(2,1)}) %all-gather.2.cloned.1.call-update) | async-done | bytes 4718608 | tf_op jit(solution)/shard_map/all_gather | solution.py:94
  290.0 12.7 %add_convert_fusion = bf16[576,1536]{1,0:T(8,128)(2,1)} fusion(bf16[576,1536]{1,0:T(8,128)(2,1)S(1)} %copy-done.15, bf16[576,4096]{1,0:T(8,128)(2,1)} %all-gather.2.cloned.1.call-done, bf16[4096,1536]{1,0:T(8,128)(2,1)} %param.11, f32[1536]{0:T(1024)S(1)} %copy-done.16), kind=kOutput, calls=%fused_computation.22 | convolution fusion | flops 7251296256 | bytes 20846592 | tf_op jit(solution)/shard_map/dot_general | solution.py:93
  (36 shorter events, 0.1 us)
Async XLA Ops:
  6.5 55.4 %copy-start = (s32[32,3]{0,1:T(4,128)S(1)}, s32[32,3]{0,1:T(4,128)}, u32[]{:S(2)}) copy-start(s32[32,3]{0,1:T(4,128)} %param.13) | copy-start | bytes 1156
  6.5 6.7 %copy-start.7 = (bf16[144,4096]{1,0:T(8,128)(2,1)S(1)}, bf16[144,4096]{1,0:T(8,128)(2,1)}, u32[]{:S(2)}) copy-start(bf16[144,4096]{1,0:T(8,128)(2,1)} %param.10) | copy-start | bytes 3538948
  9.1 20.1 %all-to-all-start.1 = ((bf16[144,4,1024]{2,0,1:T(8,128)(2,1)}), bf16[144,4,1024]{2,0,1:T(8,128)(2,1)S(1)}, u32[]{:S(2)}, u32[]{:S(2)}) async-start(bf16[144,4,1024]{2,0,1:T(8,128)(2,1)} %bitcast.60), calls=%async_computation.1 | async-start | bytes 2359296 | tf_op jit(solution)/shard_map/all_to_all | solution.py:44
  13.3 19.4 %copy-start.8 = (bf16[144,4096]{1,0:T(8,128)(2,1)S(1)}, bf16[144,4096]{1,0:T(8,128)(2,1)}, u32[]{:S(2)}) copy-start(bf16[144,4096]{1,0:T(8,128)(2,1)} %param.8) | copy-start | bytes 3538948
  29.1 19.4 %all-to-all-start = ((bf16[144,4,1024]{2,0,1:T(8,128)(2,1)}), bf16[144,4,1024]{2,0,1:T(8,128)(2,1)S(1)}, u32[]{:S(2)}, u32[]{:S(2)}) async-start(bf16[144,4,1024]{2,0,1:T(8,128)(2,1)} %bitcast.59), calls=%async_computation | async-start | bytes 2359296 | tf_op jit(solution)/shard_map/all_to_all | solution.py:45
  48.5 19.4 %all-to-all-start.2 = ((bf16[144,4,1024]{2,0,1:T(8,128)(2,1)}), bf16[144,4,1024]{2,0,1:T(8,128)(2,1)S(1)}, u32[]{:S(2)}, u32[]{:S(2)}) async-start(bf16[144,4,1024]{2,0,1:T(8,128)(2,1)} %bitcast.61), calls=%async_computation.2 | async-start | bytes 2359296 | tf_op jit(solution)/shard_map/all_to_all | solution.py:43
  52.0 237.9 %all-gather.2.cloned.1.call-start = ((), (), s32[]{:S(2)}) async-start(), calls=%async_computation.3 | async-start | bytes 5898240 | tf_op jit(solution)/shard_map/all_gather | solution.py:94
  53.7 56.3 %collective-permute-start.1 = (bf16[2,576,1024]{2,1,0:T(8,128)(2,1)}, bf16[2,576,1024]{2,1,0:T(8,128)(2,1)}, u32[]{:S(2)}, u32[]{:S(2)}) collective-permute-start(bf16[2,576,1024]{2,1,0:T(8,128)(2,1)} %pad_maximum_fusion), channel_id=1, source_target_pairs={{4,0},{8,4},{12,8},{16,12},{20,16},{24,20},{28,24},{5,1},{9,5},{13... | collective-permute-start | bytes 7077896 | tf_op jit(solution)/shard_map/ppermute | solution.py:16
  55.7 105.1 %collective-permute-start = (bf16[2,576,1024]{2,1,0:T(8,128)(2,1)}, bf16[2,576,1024]{2,1,0:T(8,128)(2,1)}, u32[]{:S(2)}, u32[]{:S(2)}) collective-permute-start(bf16[2,576,1024]{2,1,0:T(8,128)(2,1)} %pad_maximum_fusion), channel_id=1, source_target_pairs={{0,4},{4,8},{8,12},{12,16},{16,20},{20,24},{24,28},{1,5},{5,9},{9,... | collective-permute-start | bytes 7077896 | tf_op jit(solution)/shard_map/ppermute | solution.py:16
  63.1 6.0 %copy-start.11 = (s32[8]{0:T(128)}, s32[8]{0:T(128)S(1)}, u32[]{:S(2)}) copy-start(s32[8]{0:T(128)S(1)} %get-tuple-element.12) | copy-start | bytes 100
  68.5 1.4 copy-start.2
  68.6 1.8 copy-start.3
  68.6 2.2 copy-start.6
  68.6 2.2 copy-start.13
  68.6 2.2 copy-start.14
  68.6 2.2 copy-start.17
  163.2 1.4 copy-start.5
  163.2 1.4 copy-start.10
  163.2 1.4 copy-start.12
  164.6 8.1 %copy-start.4 = (s32[576,576]{1,0:T(8,128)S(1)}, s32[576,576]{1,0:T(8,128)}, u32[]{:S(2)}) copy-start(s32[576,576]{1,0:T(8,128)} %get-tuple-element.11) | copy-start | bytes 3981316
  164.6 8.1 %copy-start.9 = (pred[576]{0:T(1024)(128)(4,1)S(1)}, pred[576]{0:T(1024)(128)(4,1)}, u32[]{:S(2)}) copy-start(pred[576]{0:T(1024)(128)(4,1)} %get-tuple-element.22) | copy-start | bytes 1732
  246.1 43.9 %copy-start.15 = (bf16[576,1536]{1,0:T(8,128)(2,1)S(1)}, bf16[576,1536]{1,0:T(8,128)(2,1)}, u32[]{:S(2)}) copy-start(bf16[576,1536]{1,0:T(8,128)(2,1)} %param.7) | copy-start | bytes 5308420
  246.1 43.9 %copy-start.16 = (f32[1536]{0:T(1024)S(1)}, f32[1536]{0:T(1024)}, u32[]{:S(2)}) copy-start(f32[1536]{0:T(1024)} %param.12) | copy-start | bytes 18436
  290.0 12.7 %copy-start.1 = (s32[32,3]{0,1:T(4,128)S(1)}, s32[32,3]{0,1:T(4,128)}, u32[]{:S(2)}) copy-start(s32[32,3]{0,1:T(4,128)} %param.13) | copy-start | bytes 1156
Sparse Core Ops, SparseCore 0:
  249.0 40.9 all-gather.1
where the time goes:
time: 311 us; the launch traced here: 310 us
  waiting for transfers between devices  149 us (48%)
  local copies, waits for them, and re-layouts  54.1 us (17%)
  matrix products  51.5 us (17%)
  other arithmetic  22.3 us (7%)
  starting transfers between devices  18.8 us (6%)
  between operations  13.6 us (4%)
    ppermute x2, waiting for transfers between devices, passed_along(): return lax.ppermute(value, axis, pairs)  78.7 us
    all_gather x1, waiting for transfers between devices, shards(): lax.all_gather(head_out, 'tensor', axis=1, tiled=True)  41.1 us
    concatenate x1, local copies, waits for them, and re-layouts, shards(): jnp.concatenate([own_scores] + [part_scores(pair_rows, key_place) for pai...  36.3 us
    dot_general x3, matrix products, part_scores(): jnp.einsum('qhd,khd->hqk', query_tiles, key_tiles, preferred_element_type...  24.5 us
    all_to_all x1, waiting for transfers between devices, shards(): lax.all_to_all(key_rows, 'tensor', split_axis=1, concat_axis=0, tiled=True)  14.7 us
    all_to_all x1, waiting for transfers between devices, shards(): lax.all_to_all(value_rows, 'tensor', split_axis=1, concat_axis=0, tiled=T...  14.7 us
    dot_general x1, matrix products, shards(): jnp.einsum('hqk,khd->qhd', weights, value_all.reshape(-1, heads_here, hea...  14.3 us
    reduce_sum x1, other arithmetic, shards(): row_sum = jnp.sum(exp_scores, axis=-1, keepdims=True)  14.1 us
  transfers between devices with their start and end apart: 6, of which 5 were waited for; matrix products, arithmetic and copies ran while one was open for 7% of the time, Pallas kernels for 0%

commit v1 on v0

--- a/solution.py
+++ b/solution.py
@@ -8,6 +8,35 @@
 TILE = 32
 HT_DEV = 2
 WT = 3
+
+
+def _save_shards(on_dim, across, row_data):
+    res, t_next, z2 = (
+        lax.psum(1, axis_name=across),
+        lax.axis_index(across),
+        row_data.shape[on_dim],
+    )
+    by_place = [(src_i, (src_i + 1) % res) for src_i in range(res)]
+    pages = [(src_i, (src_i - 1) % res) for src_i in range(res)]
+    current_value = jnp.zeros(
+        (*row_data.shape[:on_dim], res * z2, *row_data.shape[on_dim + 1 :]), row_data.dtype
+    )
+    current_value = lax.dynamic_update_slice_in_dim(
+        current_value, row_data, t_next * z2, axis=on_dim
+    )
+    left_arr = g_now = row_data
+    taken_in = res // 2
+    for jj in range(1, taken_in + 1):
+        left_arr = lax.ppermute(left_arr, axis_name=across, perm=by_place)
+        current_value = lax.dynamic_update_slice_in_dim(
+            current_value, left_arr, (t_next - jj) % res * z2, axis=on_dim
+        )
+        if jj < res - taken_in:
+            g_now = lax.ppermute(g_now, axis_name=across, perm=pages)
+            current_value = lax.dynamic_update_slice_in_dim(
+                current_value, g_now, (t_next + jj) % res * z2, axis=on_dim
+            )
+    return current_value
 
 
 def passed_along(value, axis, by):
@@ -91,9 +120,7 @@
     )
     head_out = attended.reshape(tokens, inner_dev).astype(jnp.bfloat16)
     projected = jnp.dot(
-        lax.all_gather(head_out, "tensor", axis=1, tiled=True),
-        w_out,
-        preferred_element_type=jnp.float32,
+        _save_shards(1, "tensor", head_out), w_out, preferred_element_type=jnp.float32
     )
     return (residual.astype(jnp.float32) + out_gate * projected).astype(jnp.bfloat16)
 

time: 311 us -> 299 us (0.961)
  between operations: 13.6 us -> 0.34 us
    all_gather x1 -> x0, waiting for transfers between devices: 41.1 us -> none  [shards(): lax.all_gather(head_out, 'tensor', axis=1, tiled=True)]
    ppermute x0 -> x3, waiting for transfers between devices: none -> 37 us  [the longest x2 36.9 us: _save_shards(): left_arr = lax.ppermute(left_arr, axis_name=across, perm=by_place)]
    unnamed x45 -> x47, local copies, waits for them, and re-layouts: 9.07 us -> 8.81 us
  transfers between devices with their start and end apart: 6 -> 8, of which waited for: 5 -> 6; matrix products, arithmetic and copies ran while one was open for 7% -> 8% of each run, Pallas kernels for 0% -> 0%
where the time goes in v1:
time: 299 us; the launch traced here: 294 us
  waiting for transfers between devices  146 us (49%)
  local copies, waits for them, and re-layouts  56.1 us (19%)
  matrix products  49.4 us (17%)
  other arithmetic  21.7 us (7%)
  starting transfers between devices  21.4 us (7%)
    ppermute x2, waiting for transfers between devices, passed_along(): return lax.ppermute(value, axis, pairs)  79.2 us
    ppermute x2, waiting for transfers between devices, _save_shards(): left_arr = lax.ppermute(left_arr, axis_name=across, perm=by_place)  36.9 us
    concatenate x1, local copies, waits for them, and re-layouts, shards(): jnp.concatenate([own_scores] + [part_scores(pair_rows, key_place) for pai...  36.4 us
    dot_general x3, matrix products, part_scores(): jnp.einsum('qhd,khd->hqk', query_tiles, key_tiles, preferred_element_type...  24.4 us
    all_to_all x1, waiting for transfers between devices, shards(): lax.all_to_all(key_rows, 'tensor', split_axis=1, concat_axis=0, tiled=True)  14.7 us
    all_to_all x1, waiting for transfers between devices, shards(): lax.all_to_all(value_rows, 'tensor', split_axis=1, concat_axis=0, tiled=T...  14.7 us
    reduce_sum x1, other arithmetic, shards(): row_sum = jnp.sum(exp_scores, axis=-1, keepdims=True)  14.1 us
    dot_general x1, matrix products, shards(): jnp.einsum('hqk,khd->qhd', weights, value_all.reshape(-1, heads_here, hea...  13.5 us
  transfers between devices with their start and end apart: 8, of which 6 were waited for; matrix products, arithmetic and copies ran while one was open for 8% of the time, Pallas kernels for 0%

profile of v1, /device:TPU:0, one launch (start us, length us, event | category | flops | bytes accessed | tf_op | source)
XLA Modules:
  0.0 294.5 jit_solution(1346079492995851964)
XLA Ops:
  0.0 2.5 copy.94
  2.5 4.2 %all-to-all-start.1 = ((bf16[144,4,1024]{2,0,1:T(8,128)(2,1)}), bf16[144,4,1024]{2,0,1:T(8,128)(2,1)S(1)}, u32[]{:S(2)}, u32[]{:S(2)}) async-start(bf16[144,4,1024]{2,0,1:T(8,128)(2,1)} %bitcast.62), calls=%async_computation.1 | async-start | bytes 2359296 | tf_op jit(solution)/shard_map/all_to_all | solution.py:73
  6.7 1.1 copy.93
  7.9 14.7 %all-to-all-done.1 = bf16[144,4,1024]{2,0,1:T(8,128)(2,1)S(1)} async-done(((bf16[144,4,1024]{2,0,1:T(8,128)(2,1)}), bf16[144,4,1024]{2,0,1:T(8,128)(2,1)S(1)}, u32[]{:S(2)}, u32[]{:S(2)}) %all-to-all-start.1) | async-done | bytes 1179680 | tf_op jit(solution)/shard_map/all_to_all | solution.py:73
  22.6 3.5 %all-to-all-start = ((bf16[144,4,1024]{2,0,1:T(8,128)(2,1)}), bf16[144,4,1024]{2,0,1:T(8,128)(2,1)S(1)}, u32[]{:S(2)}, u32[]{:S(2)}) async-start(bf16[144,4,1024]{2,0,1:T(8,128)(2,1)} %bitcast.61), calls=%async_computation | async-start | bytes 2359296 | tf_op jit(solution)/shard_map/all_to_all | solution.py:74
  26.2 1.1 copy.95
  27.3 14.7 %all-to-all-done = bf16[144,4,1024]{2,0,1:T(8,128)(2,1)S(1)} async-done(((bf16[144,4,1024]{2,0,1:T(8,128)(2,1)}), bf16[144,4,1024]{2,0,1:T(8,128)(2,1)S(1)}, u32[]{:S(2)}, u32[]{:S(2)}) %all-to-all-start) | async-done | bytes 1179680 | tf_op jit(solution)/shard_map/all_to_all | solution.py:74
  42.0 3.5 %all-to-all-start.2 = ((bf16[144,4,1024]{2,0,1:T(8,128)(2,1)}), bf16[144,4,1024]{2,0,1:T(8,128)(2,1)S(1)}, u32[]{:S(2)}, u32[]{:S(2)}) async-start(bf16[144,4,1024]{2,0,1:T(8,128)(2,1)} %bitcast.63), calls=%async_computation.2 | async-start | bytes 2359296 | tf_op jit(solution)/shard_map/all_to_all | solution.py:72
  45.5 1.6 pad_maximum_fusion
  47.1 1.3 collective-permute-start.1
  48.4 0.6 compare_and_fusion.6
  49.1 6.2 %collective-permute-start = (bf16[2,576,1024]{2,1,0:T(8,128)(2,1)}, bf16[2,576,1024]{2,1,0:T(8,128)(2,1)}, u32[]{:S(2)}, u32[]{:S(2)}) collective-permute-start(bf16[2,576,1024]{2,1,0:T(8,128)(2,1)} %pad_maximum_fusion), channel_id=1, source_target_pairs={{0,4},{4,8},{8,12},{12,16},{16,20},{20,24},{24,28},{1,5},{5,9},{9,... | collective-permute-start | bytes 7077896 | tf_op jit(solution)/shard_map/ppermute | solution.py:45
  55.4 0.6 compare_and_fusion.8
  55.9 0.6 slice_bitcast_fusion.5
  56.6 2.0 subtract_abs_fusion.2
  58.6 2.7 subtract_abs_fusion
  61.3 0.3 copy.55
  61.7 0.3 copy.56
  62.1 0.3 copy.59
  62.4 0.2 copy.39
  62.5 0.8 copy-done.2
  63.4 0.4 copy-done.3
  63.8 0.4 copy-done.6
  64.3 8.3 %fusion.36 = (f32[8,576]{1,0:T(8,128)S(1)}, f32[8,576,576]{2,1,0:T(8,128)}) fusion(bf16[576,8,128]{2,1,0:T(8,128)(2,1)S(1)} %bitcast.80, bf16[576,8,128]{2,1,0:T(8,128)(2,1)S(1)} %bitcast.75, pred[576]{0:T(1024)(128)(4,1)S(1)} %copy-done.18, s32[8]{0:T(128)S(1)} %copy-done.14, s32[576,576]{1,0:T(8,128)S(1)} %copy-done.2, s32[8]{0:T(128)S(1)} %get-tuple-element.12, ...), kind=kOutput, calls=%fused_computation.87 | convolution fusion | flops 703360512 | bytes 16976544 | tf_op jit(solution)/shard_map/qhd,khd->hqk/dot_general | solution.py:91
  72.6 30.9 %collective-permute-done.1 = bf16[2,576,1024]{2,1,0:T(8,128)(2,1)} collective-permute-done((bf16[2,576,1024]{2,1,0:T(8,128)(2,1)}, bf16[2,576,1024]{2,1,0:T(8,128)(2,1)}, u32[]{:S(2)}, u32[]{:S(2)}) %collective-permute-start.1) | collective-permute-done | bytes 2359328 | tf_op jit(solution)/shard_map/ppermute | solution.py:45
  103.5 2.1 slice_bitcast_fusion.2
  105.6 0.3 copy.58
  105.9 48.3 %collective-permute-done = bf16[2,576,1024]{2,1,0:T(8,128)(2,1)} collective-permute-done((bf16[2,576,1024]{2,1,0:T(8,128)(2,1)}, bf16[2,576,1024]{2,1,0:T(8,128)(2,1)}, u32[]{:S(2)}, u32[]{:S(2)}) %collective-permute-start) | collective-permute-done | bytes 2359328 | tf_op jit(solution)/shard_map/ppermute | solution.py:45
  154.2 2.1 slice_bitcast_fusion.3
  156.3 0.3 copy.57
  156.6 0.3 copy.60
  157.2 0.3 copy.61
  157.5 1.2 copy.41
  158.7 8.1 %fusion.35 = (f32[8,576]{1,0:T(8,128)S(1)}, f32[8,576,576]{2,1,0:T(8,128)}) fusion(bf16[576,8,128]{2,1,0:T(8,128)(2,1)S(1)} %bitcast.76, bf16[576,8,128]{2,1,0:T(8,128)(2,1)S(1)} %bitcast.79, pred[576]{0:T(1024)(128)(4,1)S(1)} %copy-done.11, s32[8]{0:T(128)S(1)} %copy-done.14, s32[576,576]{1,0:T(8,128)S(1)} %copy-done.2, s32[8]{0:T(128)S(1)} %copy-done.13, ...), kind=kOutput, calls=%fused_computation.86 | convolution fusion | flops 703360512 | bytes 16976544 | tf_op jit(solution)/shard_map/qhd,khd->hqk/dot_general | solution.py:91
  166.8 8.1 %fusion.37 = (f32[8,576]{1,0:T(8,128)S(1)}, f32[8,576,576]{2,1,0:T(8,128)}) fusion(bf16[576,8,128]{2,1,0:T(8,128)(2,1)S(1)} %bitcast.77, bf16[576,8,128]{2,1,0:T(8,128)(2,1)S(1)} %bitcast.78, pred[576]{0:T(1024)(128)(4,1)S(1)} %copy-done.10, s32[8]{0:T(128)S(1)} %copy-done.14, s32[576,576]{1,0:T(8,128)S(1)} %copy-done.2, s32[8]{0:T(128)S(1)} %copy-done.13, ...), kind=kOutput, calls=%fused_computation.88 | convolution fusion | flops 703360512 | bytes 16976544 | tf_op jit(solution)/shard_map/qhd,khd->hqk/dot_general | solution.py:91
  174.9 36.4 %concatenate.17 = f32[8,576,1728]{2,1,0:T(8,128)} concatenate(f32[8,576,576]{2,1,0:T(8,128)} %get-tuple-element.18, f32[8,576,576]{2,1,0:T(8,128)} %get-tuple-element.20, f32[8,576,576]{2,1,0:T(8,128)} %get-tuple-element.16), dimensions={2} | concatenate | bytes 63700992 | tf_op jit(solution)/shard_map/concatenate | solution.py:104
  211.3 0.6 copy-done.9
  211.8 14.1 %fusion = f32[8,576]{1,0:T(8,128)} fusion(f32[8,576,1728]{2,1,0:T(8,128)} %concatenate.17, f32[8,576]{1,0:T(8,128)S(1)} %maximum_maximum_fusion), kind=kLoop, calls=%fused_computation.2 | loop fusion | flops 15920640 | bytes 31887360 | tf_op jit(solution)/shard_map/reduce_sum | solution.py:113
  225.9 13.5 %fusion.13 = bf16[8,72,8,128]{3,2,1,0:T(8,128)(2,1)S(1)} fusion(bf16[576,8,128]{2,0,1:T(8,128)(2,1)} %copy.41, bf16[576,8,128]{2,0,1:T(8,128)(2,1)S(1)} %copy.40, bf16[576,8,128]{2,0,1:T(8,128)(2,1)S(1)} %copy.39, f32[8,576,1728]{2,1,0:T(8,128)} %concatenate.17, f32[8,576]{1,0:T(8,128)} %fusion, f32[8,576]{1,0:T(8,128)} %copy-done.9), kind=kOutput, calls=%fused_computation.30 | convolution fusion | flops 2073526272 | bytes 36605952 | tf_op jit(solution)/shard_map/hqk,khd->qhd/dot_general | solution.py:115
  239.4 1.3 copy.92
  240.8 1.7 collective-permute-start.3
  242.5 24.7 %collective-permute-done.2 = bf16[576,1024]{1,0:T(8,128)(2,1)S(1)} collective-permute-done((bf16[576,1024]{1,0:T(8,128)(2,1)}, bf16[576,1024]{1,0:T(8,128)(2,1)S(1)}, u32[]{:S(2)}, u32[]{:S(2)}) %collective-permute-start.2) | collective-permute-done | bytes 1179680 | tf_op jit(solution)/shard_map/ppermute | solution.py:30
  267.2 0.8 collective-permute-start.4
  268.1 0.6 broadcast_in_dim.7
  268.6 0.3 constant_dynamic-update-slice_fusion.3
  269.1 1.5 constant_dynamic-update-slice_fusion.1
  270.6 12.2 %collective-permute-done.4 = bf16[576,1024]{1,0:T(8,128)(2,1)S(1)} collective-permute-done((bf16[576,1024]{1,0:T(8,128)(2,1)S(1)}, bf16[576,1024]{1,0:T(8,128)(2,1)S(1)}, u32[]{:S(2)}, u32[]{:S(2)}) %collective-permute-start.4) | collective-permute-done | bytes 1179680 | tf_op jit(solution)/shard_map/ppermute | solution.py:30
  283.0 11.5 %add_convert_fusion = bf16[576,1536]{1,0:T(8,128)(2,1)} fusion(bf16[576,1536]{1,0:T(8,128)(2,1)S(1)} %copy-done.16, bf16[576,4096]{1,0:T(8,128)(2,1)S(1)} %constant_dynamic-update-slice_fusion, bf16[4096,1536]{1,0:T(8,128)(2,1)} %param.11, f32[1536]{0:T(1024)S(1)} %copy-done.17), kind=kOutput, calls=%fused_computation.22 | convolution fusion | flops 7251296256 | bytes 20846592 | tf_op jit(solution)/shard_map/dot_general | solution.py:122
  (46 shorter events, 0.7 us)
Async XLA Ops:
  0.0 55.3 %copy-start = (s32[32,3]{0,1:T(4,128)S(1)}, s32[32,3]{0,1:T(4,128)}, u32[]{:S(2)}) copy-start(s32[32,3]{0,1:T(4,128)} %param.13) | copy-start | bytes 1156
  0.0 6.7 %copy-start.7 = (bf16[144,4096]{1,0:T(8,128)(2,1)S(1)}, bf16[144,4096]{1,0:T(8,128)(2,1)}, u32[]{:S(2)}) copy-start(bf16[144,4096]{1,0:T(8,128)(2,1)} %param.10) | copy-start | bytes 3538948
  2.5 20.1 %all-to-all-start.1 = ((bf16[144,4,1024]{2,0,1:T(8,128)(2,1)}), bf16[144,4,1024]{2,0,1:T(8,128)(2,1)S(1)}, u32[]{:S(2)}, u32[]{:S(2)}) async-start(bf16[144,4,1024]{2,0,1:T(8,128)(2,1)} %bitcast.62), calls=%async_computation.1 | async-start | bytes 2359296 | tf_op jit(solution)/shard_map/all_to_all | solution.py:73
  6.7 19.4 %copy-start.8 = (bf16[144,4096]{1,0:T(8,128)(2,1)S(1)}, bf16[144,4096]{1,0:T(8,128)(2,1)}, u32[]{:S(2)}) copy-start(bf16[144,4096]{1,0:T(8,128)(2,1)} %param.8) | copy-start | bytes 3538948
  22.6 19.4 %all-to-all-start = ((bf16[144,4,1024]{2,0,1:T(8,128)(2,1)}), bf16[144,4,1024]{2,0,1:T(8,128)(2,1)S(1)}, u32[]{:S(2)}, u32[]{:S(2)}) async-start(bf16[144,4,1024]{2,0,1:T(8,128)(2,1)} %bitcast.61), calls=%async_computation | async-start | bytes 2359296 | tf_op jit(solution)/shard_map/all_to_all | solution.py:74
  42.0 19.4 %all-to-all-start.2 = ((bf16[144,4,1024]{2,0,1:T(8,128)(2,1)}), bf16[144,4,1024]{2,0,1:T(8,128)(2,1)S(1)}, u32[]{:S(2)}, u32[]{:S(2)}) async-start(bf16[144,4,1024]{2,0,1:T(8,128)(2,1)} %bitcast.63), calls=%async_computation.2 | async-start | bytes 2359296 | tf_op jit(solution)/shard_map/all_to_all | solution.py:72
  47.1 56.3 %collective-permute-start.1 = (bf16[2,576,1024]{2,1,0:T(8,128)(2,1)}, bf16[2,576,1024]{2,1,0:T(8,128)(2,1)}, u32[]{:S(2)}, u32[]{:S(2)}) collective-permute-start(bf16[2,576,1024]{2,1,0:T(8,128)(2,1)} %pad_maximum_fusion), channel_id=1, source_target_pairs={{4,0},{8,4},{12,8},{16,12},{20,16},{24,20},{28,24},{5,1},{9,5},{13... | collective-permute-start | bytes 7077896 | tf_op jit(solution)/shard_map/ppermute | solution.py:45
  49.1 105.1 %collective-permute-start = (bf16[2,576,1024]{2,1,0:T(8,128)(2,1)}, bf16[2,576,1024]{2,1,0:T(8,128)(2,1)}, u32[]{:S(2)}, u32[]{:S(2)}) collective-permute-start(bf16[2,576,1024]{2,1,0:T(8,128)(2,1)} %pad_maximum_fusion), channel_id=1, source_target_pairs={{0,4},{4,8},{8,12},{12,16},{16,20},{20,24},{24,28},{1,5},{5,9},{9,... | collective-permute-start | bytes 7077896 | tf_op jit(solution)/shard_map/ppermute | solution.py:45
  56.6 6.0 %copy-start.12 = (s32[8]{0:T(128)}, s32[8]{0:T(128)S(1)}, u32[]{:S(2)}) copy-start(s32[8]{0:T(128)S(1)} %get-tuple-element.12) | copy-start | bytes 100
  62.0 1.4 copy-start.2
  62.0 1.8 copy-start.3
  62.0 2.2 copy-start.6
  62.0 2.2 copy-start.14
  62.0 2.2 copy-start.15
  62.0 2.2 copy-start.18
  157.1 1.6 copy-start.5
  157.1 1.6 copy-start.11
  157.1 1.5 copy-start.13
  158.7 8.1 %copy-start.4 = (s32[576,576]{1,0:T(8,128)S(1)}, s32[576,576]{1,0:T(8,128)}, u32[]{:S(2)}) copy-start(s32[576,576]{1,0:T(8,128)} %get-tuple-element.11) | copy-start | bytes 3981316
  158.7 8.1 %copy-start.10 = (pred[576]{0:T(1024)(128)(4,1)S(1)}, pred[576]{0:T(1024)(128)(4,1)}, u32[]{:S(2)}) copy-start(pred[576]{0:T(1024)(128)(4,1)} %get-tuple-element.22) | copy-start | bytes 1732
  211.2 0.6 copy-start.9
  240.8 26.4 %collective-permute-start.2 = (bf16[576,1024]{1,0:T(8,128)(2,1)}, bf16[576,1024]{1,0:T(8,128)(2,1)S(1)}, u32[]{:S(2)}, u32[]{:S(2)}) collective-permute-start(bf16[576,1024]{1,0:T(8,128)(2,1)} %bitcast.60), channel_id=1, source_target_pairs={{0,1},{1,2},{2,3},{3,0},{4,5},{5,6},{6,7},{7,4},{8,9},{9,10},{10,1... | collective-permute-start | bytes 3538952 | tf_op jit(solution)/shard_map/ppermute | solution.py:30
  240.8 28.2 %collective-permute-start.3 = (bf16[576,1024]{1,0:T(8,128)(2,1)}, bf16[576,1024]{1,0:T(8,128)(2,1)}, u32[]{:S(2)}, u32[]{:S(2)}) collective-permute-start(bf16[576,1024]{1,0:T(8,128)(2,1)} %bitcast.60), channel_id=1, source_target_pairs={{0,3},{1,0},{2,1},{3,2},{4,7},{5,4},{6,5},{7,6},{8,11},{9,8},{10,9... | collective-permute-start | bytes 3538952 | tf_op jit(solution)/shard_map/ppermute | solution.py:35
  267.2 15.6 %collective-permute-start.4 = (bf16[576,1024]{1,0:T(8,128)(2,1)S(1)}, bf16[576,1024]{1,0:T(8,128)(2,1)S(1)}, u32[]{:S(2)}, u32[]{:S(2)}) collective-permute-start(bf16[576,1024]{1,0:T(8,128)(2,1)S(1)} %collective-permute-done.2), channel_id=1, source_target_pairs={{0,1},{1,2},{2,3},{3,0},{4,5},{5,6},{6,7},{7,4},{8,9},{9,10},{10,1... | collective-permute-start | bytes 3538952 | tf_op jit(solution)/shard_map/ppermute | solution.py:30
  269.0 14.0 %copy-start.16 = (bf16[576,1536]{1,0:T(8,128)(2,1)S(1)}, bf16[576,1536]{1,0:T(8,128)(2,1)}, u32[]{:S(2)}) copy-start(bf16[576,1536]{1,0:T(8,128)(2,1)} %param.7) | copy-start | bytes 5308420
  269.1 14.0 %copy-start.17 = (f32[1536]{0:T(1024)S(1)}, f32[1536]{0:T(1024)}, u32[]{:S(2)}) copy-start(f32[1536]{0:T(1024)} %param.12) | copy-start | bytes 18436
  283.0 11.5 %copy-start.1 = (s32[32,3]{0,1:T(4,128)S(1)}, s32[32,3]{0,1:T(4,128)}, u32[]{:S(2)}) copy-start(s32[32,3]{0,1:T(4,128)} %param.13) | copy-start | bytes 1156
